TPU v7x, 256 devices: a whole 4x4x8 slice. The times are simulated.
256 devices in a mesh: dp: 64 (over z, x, core), tensor: 4 (over y).
Axes of the slice: x: 4, y: 4, z: 8, core: 2. Of those that a mesh axis runs over, the one named last changes fastest.
Arguments:
- gradients: float32 [64, 128, 3, 28672], P('dp', None, None, 'tensor'), may hold values from -2097152 to 2097152
- token_counts: int32 [64, 3], P('dp'), may hold values from 512 to 6143
- modality: int32 [64], P('dp'), may hold values from 0 to 2
- loss_weight: float32 [3], replicated, may hold values from 0.5 to 2
- master: float32 [128, 3, 28672], P('dp', None, 'tensor'), may hold values from -6 to 6
- moment_one: float32 [128, 3, 28672], P('dp', None, 'tensor'), may hold values from -6 to 6
- moment_two: float32 [128, 3, 28672], P('dp', None, 'tensor'), may hold values from 0.05 to 2
Outputs:
- new_master: float32 [128, 3, 28672], P('dp', None, 'tensor')
- new_moment_one: float32 [128, 3, 28672], P('dp', None, 'tensor')
- new_moment_two: float32 [128, 3, 28672], P('dp', None, 'tensor')
- working_weights: bfloat16 [128, 3, 28672], P(None, None, 'tensor')
Inputs may be any that keep to these rules, and one draw needn't show every extreme that they name: `modality`: 0 is text, 1 image, 2 audio.
All inputs are finite; a program needn't handle non-finite values.
Results may differ from a plain program's by a relative error of at most 0.001.
Values may be sent and summed in bfloat16 or wider, within the bound.
No kernel may reach another device: no remote copies, remote signals or barrier semaphores. Data moves between devices by JAX's collectives and lax.ppermute only.
A program may use at most 128 MiB of HBM per device.

v0:
```python
import jax
import jax.numpy as jnp
from jax import lax
from jax.sharding import Mesh
from jax.sharding import PartitionSpec as P

DP = ("dp_0", "dp_1", "dp_2")
beta_one = 0.9
beta_two = 0.95
bias_one = 1.0 - 0.9**10
bias_two = 1.0 - 0.95**10
epsilon = 1e-08
learn_rate = 0.01
decay_rate = 0.1


def in_order(parts, dim):
    parts = jnp.moveaxis(parts, 0, dim)
    dims = parts.shape
    return parts.reshape(*dims[:dim], dims[dim] * dims[dim + 1], *dims[dim + 2 :])


def all_blocks(value, axes, turns):
    parts = value[None]
    for k in turns:
        parts = lax.all_gather(parts, axes[k], axis=0, tiled=True)
    current = [lax.axis_size(axes[k]) for k in reversed(turns)]
    parts = parts.reshape(*current, *value.shape)
    turned = sorted(range(len(turns)), key=lambda place: turns[len(turns) - 1 - place])
    return parts.transpose(*turned, *range(len(turns), parts.ndim)).reshape(-1, *value.shape)


def gather_axes(value, axes, turns, dim):
    return in_order(all_blocks(value, axes, turns), dim)


def from_everyone(value, axis):
    devices = lax.axis_size(axis)
    return lax.all_to_all(
        jnp.broadcast_to(value[None], (devices, *value.shape)), axis, 0, 0, tiled=True
    )


def taken_together(value, axis):
    return from_everyone(value, axis).sum(axis=0)


def scatter_axes(value, axes, dim):
    if not axes:
        return value
    nearer = lax.psum_scatter(value, axes[0], scatter_dimension=dim, tiled=True)
    return scatter_axes(nearer, axes[1:], dim)


def adam_update(grad_sum, first, second, weights):
    first_new = beta_one * first + (1.0 - beta_one) * grad_sum
    second_new = beta_two * second + (1.0 - beta_two) * grad_sum * grad_sum
    step_size = first_new / bias_one / (jnp.sqrt(second_new / bias_two) + epsilon)
    weights_new = weights - learn_rate * (step_size + decay_rate * weights)
    return (weights_new, first_new, second_new)


def publish(weights_new):
    return gather_axes(weights_new.astype(jnp.bfloat16), DP, (1, 0, 2), 0)


def local(gradients, token_counts, modality, loss_weight, master, moment_one, moment_two):
    totals = taken_together(token_counts[0], DP).astype(jnp.float32)
    ratios = loss_weight / totals
    picked = (lax.iota(jnp.int32, 3) == modality[0]).astype(jnp.float32)
    own_scale = jnp.sum(picked * ratios)
    replica_grad = gradients[0]
    summed = scatter_axes(replica_grad * own_scale, DP, 0)
    weights_new, first_new, second_new = adam_update(summed, moment_one, moment_two, master)
    return (weights_new, first_new, second_new, publish(weights_new))


def solution(mesh):
    torus = Mesh(
        mesh.devices.reshape(8, 4, 2, mesh.shape["tensor"]), ("dp_0", "dp_1", "dp_2", "tensor")
    )
    in_specs = (
        P(DP, None, None, "tensor"),
        P(DP, None),
        P(DP),
        P(),
        P(DP, None, "tensor"),
        P(DP, None, "tensor"),
        P(DP, None, "tensor"),
    )
    out_specs = (
        P(DP, None, "tensor"),
        P(DP, None, "tensor"),
        P(DP, None, "tensor"),
        P(None, None, "tensor"),
    )
    return jax.shard_map(local, mesh=torus, in_specs=in_specs, out_specs=out_specs, check_vma=False)
```

profile of v0, /device:TPU:1, one launch (start us, length us, event | category | flops | bytes accessed | tf_op | source)
XLA Modules:
  0.0 351.3 jit_solution(10869749909884527604)
XLA Ops:
  7.2 1.3 broadcast_in_dim.8
  8.5 13.0 %all-to-all-start = ((s32[64,1,3]{2,1,0:T(1,128)}), s32[64,1,3]{2,1,0:T(1,128)S(1)}, u32[]{:S(2)}, u32[]{:S(2)}) async-start(s32[64,1,3]{2,1,0:T(1,128)} %broadcast_in_dim.8), calls=%async_computation | async-start | bytes 65536 | tf_op jit(solution)/shard_map/all_to_all | solution.py:39
  21.4 0.0 reduce-scatter.4.cloned.1.call-start
  22.1 8.6 %all-to-all-done = s32[64,1,3]{2,1,0:T(1,128)S(1)} async-done(((s32[64,1,3]{2,1,0:T(1,128)}), s32[64,1,3]{2,1,0:T(1,128)S(1)}, u32[]{:S(2)}, u32[]{:S(2)}) %all-to-all-start) | async-done | bytes 800 | tf_op jit(solution)/shard_map/all_to_all | solution.py:39
  30.8 0.1 reduce_sum.18
  30.8 1.3 fusion.1
  32.1 10.2 %multiply_bitcast_fusion = f32[128,3,7168]{2,0,1:T(8,128)} fusion(f32[1,128,3,7168]{3,1,2,0:T(8,128)} %param.7, f32[]{:T(128)} %fusion.1), kind=kLoop, calls=%fused_computation | loop fusion | flops 2752512 | bytes 22020100 | tf_op jit(solution)/shard_map/mul | solution.py:73
  42.3 0.0 copy-start.4
  42.3 0.0 copy-start.3
  42.3 0.0 copy-start
  42.3 0.0 copy-start.1
  42.3 0.0 copy-start.2
  42.3 0.0 reduce-scatter.4.cloned.1.call-update
  42.4 0.0 all-reduce.5.cloned.1.call-start
  42.4 114.5 %reduce-scatter.4.cloned.1.call-done = f32[16,3,7168]{2,0,1:T(8,128)} async-done(((f32[128,3,7168]{2,0,1:T(8,128)}), f32[16,3,7168]{2,0,1:T(8,128)}) %reduce-scatter.4.cloned.1.call-update) | async-done | bytes 1376272 | tf_op jit(solution)/shard_map/reduce_scatter | solution.py:51
  156.9 0.0 all-reduce.5.cloned.1.call-update
  156.9 0.0 all-reduce.7.cloned.1.call-start
  157.0 0.0 copy-done.4
  157.0 0.6 dynamic-slice
  158.2 52.2 %all-reduce.5.cloned.1.call-done = f32[16,3,7168]{2,0,1:T(8,128)} async-done(((f32[16,3,7168]{2,0,1:T(8,128)}), f32[16,3,7168]{2,0,1:T(8,128)}) %all-reduce.5.cloned.1.call-update) | async-done | bytes 1376272
  210.4 1.9 constant_dynamic-slice_fusion
  212.3 0.0 all-reduce.7.cloned.1.call-update
  212.3 0.0 all-gather.4.cloned.1.call-start
  212.4 0.0 copy-done.3
  212.4 0.6 dynamic-slice.2
  213.6 31.2 %all-reduce.7.cloned.1.call-done = f32[4,3,7168]{2,0,1:T(4,128)} async-done(((f32[4,3,7168]{2,0,1:T(4,128)}), f32[4,3,7168]{2,0,1:T(4,128)}) %all-reduce.7.cloned.1.call-update) | async-done | bytes 344080
  244.8 0.0 copy-done
  244.8 0.0 copy-done.1
  244.8 0.0 copy-done.2
  244.8 2.4 fusion.2
  247.2 10.5 %all-gather = bf16[8,3,7168]{2,1,0:T(4,128)(2,1)S(1)} all-gather(bf16[2,3,7168]{2,1,0:T(4,128)(2,1)S(1)} %copy.25), channel_id=2, replica_groups=mesh['dp_0'=8,'dp_1'=4,'dp_2'=2,'tensor'=4] {'dp_1'}, dimensions={0}, use_global_device_ids=true | all-gather | bytes 430080 | tf_op jit(solution)/shard_map/all_gather | solution.py:26
  257.7 1.0 copy.26
  258.8 0.0 all-gather.4.cloned.1.call-update
  258.8 0.0 all-gather.6.cloned.1.call-start
  258.8 43.1 %all-gather.4.cloned.1.call-done = bf16[32,2,3,7168]{3,1,2,0:T(2,128)(2,1)} async-done(((bf16[4,2,3,7168]{3,1,2,0:T(2,128)(2,1)}), bf16[32,2,3,7168]{3,1,2,0:T(2,128)(2,1)}) %all-gather.4.cloned.1.call-update) | async-done | bytes 2752528 | tf_op jit(solution)/shard_map/all_gather | solution.py:26
  301.9 0.0 all-gather.6.cloned.1.call-update
  301.9 24.7 %all-gather.6.cloned.1.call-done = bf16[64,2,3,7168]{3,1,2,0:T(2,128)(2,1)} async-done(((bf16[32,2,3,7168]{3,1,2,0:T(2,128)(2,1)}), bf16[64,2,3,7168]{3,1,2,0:T(2,128)(2,1)}) %all-gather.6.cloned.1.call-update) | async-done | bytes 5505040 | tf_op jit(solution)/shard_map/all_gather | solution.py:26
  326.6 6.4 %copy.27 = bf16[8,4,2,2,3,7168]{5,3,2,1,0,4:T(2,128)(2,1)} copy(bf16[8,4,2,2,3,7168]{5,3,4,1,0,2:T(2,128)(2,1)} %bitcast.13) | data formatting | bytes 11010048 | tf_op jit(solution)/shard_map/transpose | solution.py:30
  333.0 11.8 %reshape_reshape.3 = bf16[128,3,7168]{2,0,1:T(8,128)(2,1)} reshape(bf16[8,4,2,2,3,7168]{5,3,2,1,0,4:T(2,128)(2,1)} %copy.27) | data formatting | bytes 11010048 | tf_op jit(solution)/shard_map/reshape;reshape | solution.py:20
  (1 shorter events, 0.0 us)
Async XLA Ops:
  8.5 22.3 %all-to-all-start = ((s32[64,1,3]{2,1,0:T(1,128)}), s32[64,1,3]{2,1,0:T(1,128)S(1)}, u32[]{:S(2)}, u32[]{:S(2)}) async-start(s32[64,1,3]{2,1,0:T(1,128)} %broadcast_in_dim.8), calls=%async_computation | async-start | bytes 65536 | tf_op jit(solution)/shard_map/all_to_all | solution.py:39
  21.4 135.5 %reduce-scatter.4.cloned.1.call-start = ((), (), s32[]{:S(2)}) async-start(), calls=%async_computation.2 | async-start | bytes 12386304 | tf_op jit(solution)/shard_map/reduce_scatter | solution.py:51
  42.3 114.7 %copy-start.4 = (u32[256]{0:T(256)S(1)}, u32[256]{0:T(256)}, u32[]{:S(2)}) copy-start(u32[256]{0:T(256)} %constant.31) | copy-start | bytes 3076
  42.3 170.0 %copy-start.3 = (u32[256]{0:T(256)S(1)}, u32[256]{0:T(256)}, u32[]{:S(2)}) copy-start(u32[256]{0:T(256)} %constant.35) | copy-start | bytes 3076
  42.3 202.4 %copy-start = (f32[2,3,7168]{2,0,1:T(2,128)S(1)}, f32[2,3,7168]{2,0,1:T(2,128)}, u32[]{:S(2)}) copy-start(f32[2,3,7168]{2,0,1:T(2,128)} %param.11) | copy-start | bytes 516100
  42.3 202.4 %copy-start.1 = (f32[2,3,7168]{2,0,1:T(2,128)S(1)}, f32[2,3,7168]{2,0,1:T(2,128)}, u32[]{:S(2)}) copy-start(f32[2,3,7168]{2,0,1:T(2,128)} %param.12) | copy-start | bytes 516100
  42.3 202.4 %copy-start.2 = (f32[2,3,7168]{2,0,1:T(2,128)S(1)}, f32[2,3,7168]{2,0,1:T(2,128)}, u32[]{:S(2)}) copy-start(f32[2,3,7168]{2,0,1:T(2,128)} %param.13) | copy-start | bytes 516100
  42.4 168.0 %all-reduce.5.cloned.1.call-start = ((), (), s32[]{:S(2)}) async-start(), calls=%async_computation.5 | async-start | bytes 2752512
  156.9 87.8 %all-reduce.7.cloned.1.call-start = ((), (), s32[]{:S(2)}) async-start(), calls=%async_computation.6 | async-start | bytes 688128
  212.3 89.6 %all-gather.4.cloned.1.call-start = ((), (), s32[]{:S(2)}) async-start(), calls=%async_computation.3 | async-start | bytes 3096576 | tf_op jit(solution)/shard_map/all_gather | solution.py:26
  258.8 67.8 %all-gather.6.cloned.1.call-start = ((), (), s32[]{:S(2)}) async-start(), calls=%async_computation.4 | async-start | bytes 8257536 | tf_op jit(solution)/shard_map/all_gather | solution.py:26
Sparse Core Ops, SparseCore 0:
  42.5 114.3 reduce-scatter.3
  159.3 51.0 all-reduce.4
  213.6 31.1 all-reduce.6
  258.9 42.9 all-gather.3
  303.6 23.0 all-gather.5
where the time goes:
time: 352 us; the launch traced here: 351 us
  waiting for transfers between devices  274 us (78%)
  local copies, waits for them, and re-layouts  23.7 us (7%)
  between operations  15.8 us (4%)
  other arithmetic  13.9 us (4%)
  starting transfers between devices  13.2 us (4%)
  blocking collectives  10.5 us (3%)
    reduce_scatter x1, waiting for transfers between devices, scatter_axes(): nearer = lax.psum_scatter(value, axes[0], scatter_dimension=dim, tiled=True)  114 us
    unnamed x7, waiting for transfers between devices  83.4 us
    all_gather x2, waiting for transfers between devices, all_blocks(): parts = lax.all_gather(parts, axes[k], axis=0, tiled=True)  67.7 us
    all_to_all x1, starting transfers between devices, from_everyone(): lax.all_to_all(jnp.broadcast_to(value[None], (devices, *value.shape)), ax...  13 us
    another operation x1, local copies, waits for them, and re-layouts, in_order(): parts.reshape(*dims[:dim], dims[dim] * dims[dim + 1], *dims[dim + 2:])  11.8 us
    all_gather x1, blocking collectives, all_blocks(): parts = lax.all_gather(parts, axes[k], axis=0, tiled=True)  10.5 us
    mul x1, other arithmetic, local(): summed = scatter_axes(replica_grad * own_scale, DP, 0)  10.2 us
    all_to_all x1, waiting for transfers between devices, from_everyone(): lax.all_to_all(jnp.broadcast_to(value[None], (devices, *value.shape)), ax...  8.63 us
  transfers between devices with their start and end apart: 6, of which 6 were waited for; matrix products, arithmetic and copies ran while one was open for 0% of the time, Pallas kernels for 0%

commit v1 on v0

--- a/solution.py
+++ b/solution.py
@@ -23,7 +23,9 @@
 def all_blocks(value, axes, turns):
     parts = value[None]
     for k in turns:
-        parts = lax.all_gather(parts, axes[k], axis=0, tiled=True)
+        parts = jnp.concatenate(
+            lax.all_to_all(jnp.stack([parts] * lax.axis_size(axes[k])), axes[k], 0, 0), axis=0
+        )
     current = [lax.axis_size(axes[k]) for k in reversed(turns)]
     parts = parts.reshape(*current, *value.shape)
     turned = sorted(range(len(turns)), key=lambda place: turns[len(turns) - 1 - place])

time: 352 us -> 379 us (1.077)
  blocking collectives: 10.5 us -> 90.8 us
  waiting for transfers between devices: 274 us -> 207 us
  local copies, waits for them, and re-layouts: 23.7 us -> 32.2 us
  other arithmetic: 13.9 us -> 19.9 us
    all_to_all x0 -> x3, blocking collectives: none -> 90.8 us  [all_blocks(): lax.all_to_all(jnp.stack([parts] * lax.axis_size(axes[k])), axes[k], 0, 0)]
    all_gather x2 -> x0, waiting for transfers between devices: 67.7 us -> none  [all_blocks(): parts = lax.all_gather(parts, axes[k], axis=0, tiled=True)]
    all_gather x1 -> x0, blocking collectives: 10.5 us -> none  [all_blocks(): parts = lax.all_gather(parts, axes[k], axis=0, tiled=True)]
    another operation x0 -> x4, local copies, waits for them, and re-layouts: none -> 9.01 us  [all_blocks(): jnp.stack([parts] * lax.axis_size(axes[k]))]
    another operation x0 -> x1, other arithmetic: none -> 5.97 us  [all_blocks(): jnp.stack([parts] * lax.axis_size(axes[k]))]
    unnamed x7 -> x5, waiting for transfers between devices: 83.4 us -> 83.4 us
  transfers between devices with their start and end apart: 6 -> 4, of which waited for: 6 -> 4; matrix products, arithmetic and copies ran while one was open for 0% -> 0% of each run, Pallas kernels for 0% -> 0%
where the time goes in v1:
time: 379 us; the launch traced here: 378 us
  waiting for transfers between devices  207 us (55%)
  blocking collectives  90.8 us (24%)
  local copies, waits for them, and re-layouts  32.2 us (8%)
  other arithmetic  19.9 us (5%)
  between operations  15.8 us (4%)
  starting transfers between devices  13.1 us (3%)
    reduce_scatter x1, waiting for transfers between devices, scatter_axes(): nearer = lax.psum_scatter(value, axes[0], scatter_dimension=dim, tiled=True)  114 us
    all_to_all x3, blocking collectives, all_blocks(): lax.all_to_all(jnp.stack([parts] * lax.axis_size(axes[k])), axes[k], 0, 0)  90.8 us
    unnamed x5, waiting for transfers between devices  83.4 us
    all_to_all x1, starting transfers between devices, from_everyone(): lax.all_to_all(jnp.broadcast_to(value[None], (devices, *value.shape)), ax...  13 us
    another operation x1, local copies, waits for them, and re-layouts, in_order(): parts.reshape(*dims[:dim], dims[dim] * dims[dim + 1], *dims[dim + 2:])  11.8 us
    mul x1, other arithmetic, local(): summed = scatter_axes(replica_grad * own_scale, DP, 0)  10.2 us
    another operation x4, local copies, waits for them, and re-layouts, all_blocks(): jnp.stack([parts] * lax.axis_size(axes[k]))  9.01 us
    all_to_all x1, waiting for transfers between devices, from_everyone(): lax.all_to_all(jnp.broadcast_to(value[None], (devices, *value.shape)), ax...  8.63 us
  transfers between devices with their start and end apart: 4, of which 4 were waited for; matrix products, arithmetic and copies ran while one was open for 0% of the time, Pallas kernels for 0%

profile of v1, /device:TPU:1, one launch (start us, length us, event | category | flops | bytes accessed | tf_op | source)
XLA Modules:
  0.0 378.3 jit_solution(13479106348608060170)
XLA Ops:
  7.2 1.3 broadcast_in_dim.2
  8.5 13.0 %all-to-all-start = ((s32[64,1,3]{2,1,0:T(1,128)}), s32[64,1,3]{2,1,0:T(1,128)S(1)}, u32[]{:S(2)}, u32[]{:S(2)}) async-start(s32[64,1,3]{2,1,0:T(1,128)} %broadcast_in_dim.2), calls=%async_computation | async-start | bytes 65536 | tf_op jit(solution)/shard_map/all_to_all | solution.py:41
  21.4 0.0 reduce-scatter.4.cloned.1.call-start
  22.1 8.6 %all-to-all-done = s32[64,1,3]{2,1,0:T(1,128)S(1)} async-done(((s32[64,1,3]{2,1,0:T(1,128)}), s32[64,1,3]{2,1,0:T(1,128)S(1)}, u32[]{:S(2)}, u32[]{:S(2)}) %all-to-all-start) | async-done | bytes 800 | tf_op jit(solution)/shard_map/all_to_all | solution.py:41
  30.8 0.1 reduce_sum.18
  30.8 1.3 fusion.1
  32.1 10.2 %multiply_bitcast_fusion = f32[128,3,7168]{2,0,1:T(8,128)} fusion(f32[1,128,3,7168]{3,1,2,0:T(8,128)} %param.7, f32[]{:T(128)} %fusion.1), kind=kLoop, calls=%fused_computation | loop fusion | flops 2752512 | bytes 22020100 | tf_op jit(solution)/shard_map/mul | solution.py:75
  42.3 0.0 copy-start.4
  42.3 0.0 copy-start.3
  42.3 0.0 copy-start
  42.3 0.0 copy-start.1
  42.3 0.0 copy-start.2
  42.3 0.0 reduce-scatter.4.cloned.1.call-update
  42.4 0.0 all-reduce.5.cloned.1.call-start
  42.4 114.5 %reduce-scatter.4.cloned.1.call-done = f32[16,3,7168]{2,0,1:T(8,128)} async-done(((f32[128,3,7168]{2,0,1:T(8,128)}), f32[16,3,7168]{2,0,1:T(8,128)}) %reduce-scatter.4.cloned.1.call-update) | async-done | bytes 1376272 | tf_op jit(solution)/shard_map/reduce_scatter | solution.py:53
  156.9 0.0 all-reduce.5.cloned.1.call-update
  156.9 0.0 all-reduce.7.cloned.1.call-start
  157.0 0.0 copy-done.4
  157.0 0.6 dynamic-slice
  158.2 52.2 %all-reduce.5.cloned.1.call-done = f32[16,3,7168]{2,0,1:T(8,128)} async-done(((f32[16,3,7168]{2,0,1:T(8,128)}), f32[16,3,7168]{2,0,1:T(8,128)}) %all-reduce.5.cloned.1.call-update) | async-done | bytes 1376272
  210.4 1.9 constant_dynamic-slice_fusion
  212.3 0.0 all-reduce.7.cloned.1.call-update
  212.3 0.0 copy-done.3
  212.3 0.6 dynamic-slice.2
  213.6 31.2 %all-reduce.7.cloned.1.call-done = f32[4,3,7168]{2,0,1:T(4,128)} async-done(((f32[4,3,7168]{2,0,1:T(4,128)}), f32[4,3,7168]{2,0,1:T(4,128)}) %all-reduce.7.cloned.1.call-update) | async-done | bytes 344080
  244.8 0.0 copy-done
  244.8 0.0 copy-done.1
  244.8 0.0 copy-done.2
  244.8 2.4 fusion.2
  247.1 0.2 stack.9
  247.3 10.3 %all_to_all.21 = bf16[4,1,2,3,7168]{4,2,3,1,0:T(2,128)(2,1)S(1)} all-to-all(bf16[4,1,2,3,7168]{4,2,3,1,0:T(2,128)(2,1)S(1)} %stack.9), channel_id=1, replica_groups=mesh['dp_0'=8,'dp_1'=4,'dp_2'=2,'tensor'=4] {'dp_1'}, dimensions={0} | all-to-all | bytes 688128 | tf_op jit(solution)/shard_map/all_to_all | solution.py:27
  257.7 0.2 copy.27
  257.9 2.5 stack.10
  260.4 69.1 %all_to_all.22 = bf16[8,4,2,3,7168]{4,2,1,3,0:T(2,128)(2,1)S(1)} all-to-all(bf16[8,4,2,3,7168]{4,2,1,3,0:T(2,128)(2,1)S(1)} %stack.10), channel_id=1, replica_groups=mesh['dp_0'=8,'dp_1'=4,'dp_2'=2,'tensor'=4] {'dp_0'}, dimensions={0} | all-to-all | bytes 5505024 | tf_op jit(solution)/shard_map/all_to_all | solution.py:27
  329.5 2.1 copy.28
  331.6 6.0 %pad_maximum_fusion = bf16[2,32,2,3,7168]{4,2,3,1,0:T(2,128)(2,1)S(1)} fusion(bf16[1,32,2,3,7168]{4,2,3,1,0:T(2,128)(2,1)S(1)} %bitcast.15), kind=kLoop, calls=%fused_computation.1 | loop fusion | flops 2752512 | bytes 8257536 | tf_op jit(solution)/shard_map/stack | solution.py:27
  337.6 6.1 %copy.29 = bf16[2,32,2,3,7168]{4,2,1,3,0:T(2,128)(2,1)S(1)} copy(bf16[2,32,2,3,7168]{4,2,3,1,0:T(2,128)(2,1)S(1)} %pad_maximum_fusion) | data formatting | bytes 11010048 | tf_op jit(solution)/shard_map/stack | solution.py:27
  343.8 11.4 %all_to_all.23 = bf16[2,32,2,3,7168]{4,2,1,3,0:T(2,128)(2,1)S(1)} all-to-all(bf16[2,32,2,3,7168]{4,2,1,3,0:T(2,128)(2,1)S(1)} %copy.29), channel_id=1, replica_groups=mesh['dp_0'=8,'dp_1'=4,'dp_2'=2,'tensor'=4] {'dp_2'}, dimensions={0} | all-to-all | bytes 11010048 | tf_op jit(solution)/shard_map/all_to_all | solution.py:27
  355.1 4.9 %copy.30 = bf16[8,4,2,2,3,7168]{5,3,2,1,0,4:T(2,128)(2,1)} copy(bf16[8,4,2,2,3,7168]{5,3,1,0,4,2:T(2,128)(2,1)S(1)} %bitcast.14) | data formatting | bytes 11010048 | tf_op jit(solution)/shard_map/transpose | solution.py:32
  360.0 11.8 %reshape_reshape.7 = bf16[128,3,7168]{2,0,1:T(8,128)(2,1)} reshape(bf16[8,4,2,2,3,7168]{5,3,2,1,0,4:T(2,128)(2,1)} %copy.30) | data formatting | bytes 11010048 | tf_op jit(solution)/shard_map/reshape;reshape | solution.py:20
Async XLA Ops:
  8.5 22.3 %all-to-all-start = ((s32[64,1,3]{2,1,0:T(1,128)}), s32[64,1,3]{2,1,0:T(1,128)S(1)}, u32[]{:S(2)}, u32[]{:S(2)}) async-start(s32[64,1,3]{2,1,0:T(1,128)} %broadcast_in_dim.2), calls=%async_computation | async-start | bytes 65536 | tf_op jit(solution)/shard_map/all_to_all | solution.py:41
  21.4 135.5 %reduce-scatter.4.cloned.1.call-start = ((), (), s32[]{:S(2)}) async-start(), calls=%async_computation.5 | async-start | bytes 12386304 | tf_op jit(solution)/shard_map/reduce_scatter | solution.py:53
  42.3 114.7 %copy-start.4 = (u32[256]{0:T(256)S(1)}, u32[256]{0:T(256)}, u32[]{:S(2)}) copy-start(u32[256]{0:T(256)} %constant.31) | copy-start | bytes 3076
  42.3 170.0 %copy-start.3 = (u32[256]{0:T(256)S(1)}, u32[256]{0:T(256)}, u32[]{:S(2)}) copy-start(u32[256]{0:T(256)} %constant.35) | copy-start | bytes 3076
  42.3 202.4 %copy-start = (f32[2,3,7168]{2,0,1:T(2,128)S(1)}, f32[2,3,7168]{2,0,1:T(2,128)}, u32[]{:S(2)}) copy-start(f32[2,3,7168]{2,0,1:T(2,128)} %param.11) | copy-start | bytes 516100
  42.3 202.4 %copy-start.1 = (f32[2,3,7168]{2,0,1:T(2,128)S(1)}, f32[2,3,7168]{2,0,1:T(2,128)}, u32[]{:S(2)}) copy-start(f32[2,3,7168]{2,0,1:T(2,128)} %param.12) | copy-start | bytes 516100
  42.3 202.4 %copy-start.2 = (f32[2,3,7168]{2,0,1:T(2,128)S(1)}, f32[2,3,7168]{2,0,1:T(2,128)}, u32[]{:S(2)}) copy-start(f32[2,3,7168]{2,0,1:T(2,128)} %param.13) | copy-start | bytes 516100
  42.4 168.0 %all-reduce.5.cloned.1.call-start = ((), (), s32[]{:S(2)}) async-start(), calls=%async_computation.6 | async-start | bytes 2752512
  156.9 87.8 %all-reduce.7.cloned.1.call-start = ((), (), s32[]{:S(2)}) async-start(), calls=%async_computation.7 | async-start | bytes 688128
Sparse Core Ops, SparseCore 0:
  42.5 114.3 reduce-scatter.3
  159.3 51.0 all-reduce.4
  213.6 31.1 all-reduce.6
